TPU v7x, 32 devices: a whole 2x2x4 slice. The times are simulated.
32 devices in a mesh: group: 2 (over x), wide: 16 (over z, y, core).
Axes of the slice: x: 2, y: 2, z: 4, core: 2. Of those that a mesh axis runs over, the one named last changes fastest.
Arguments:
- visibilities: float32 [6144, 2, 128], P(('group', 'wide')), parts along dimension 0, may hold values from -6 to 6
- offsets: float32 [6144, 2, 128], P(('group', 'wide')), parts along dimension 0, may hold values from 2 to 30
- vis_count: int32 [6144], P(('group', 'wide')), parts along dimension 0, may hold values from 1 to 128, 294912 in all
- owner: int32 [6144], P(('group', 'wide')), parts along dimension 0, may hold values from 0 to 15, as said below
- tile_row: int32 [6144], P(('group', 'wide')), parts along dimension 0, may hold values from 0 to 7
- tile_col: int32 [6144], P(('group', 'wide')), parts along dimension 0, may hold values from 0 to 127
Outputs:
- image: float32 [2, 8192, 4096], P(None, 'group', 'wide'), parts along dimension 1
There are 2 independent parts, one for each index of `group`. A program takes and returns all parts, laid end to end along the dimension named above; each array names one. Nothing has to cross between parts.
Inputs may be any that keep to these rules, and one draw needn't show every extreme that they name: At most 36 subgrids of one device have the same owner; in every draw one owner receives exactly 36 subgrids from every device. `vis_count`: the live visibilities of a subgrid are the first ones of its slots; some subgrid has all 128 live; over each part along group the counts sum to 294912.
All inputs are finite; a program needn't handle non-finite values.
Results may differ from a plain program's by a relative error of at most 0.0003.
Values sent between devices are 32-bit elements; how exact they have to be, the bound alone decides.
A program may use at most 128 MiB of HBM per device.

v0:
```python
import math

import jax
import jax.numpy as jnp
from jax import lax
from jax.sharding import PartitionSpec as P

SUB = 32
VIS = 128
SUB_DEV = 192
GRID = 4096
FA = 128


highest = lax.Precision.HIGHEST


def cplx_einsum(pattern, left_real, left_imag, right_real, right_imag):

    def single(first, second):
        return jnp.einsum(pattern, first, second, precision=highest)

    return (
        single(left_real, right_real) - single(left_imag, right_imag),
        single(left_real, right_imag) + single(left_imag, right_real),
    )


def dft_table(length, factor):
    indices = jnp.arange(length)
    phase_int = indices[:, None] * indices[None, :] % length
    angles = -2.0 * math.pi / length * phase_int.astype(jnp.float32)
    return (jnp.cos(angles) * factor, jnp.sin(angles) * factor)


def twiddle_table():
    outer_size = GRID // FA
    phase_int = jnp.arange(outer_size)[:, None] * jnp.arange(FA)[None, :] % GRID
    angles = -2.0 * math.pi / GRID * phase_int.astype(jnp.float32)
    return (jnp.cos(angles), jnp.sin(angles))


def subgrid_spectra(samples, counts):
    subgrid_count = samples.shape[0]
    position = (jnp.arange(SUB, dtype=jnp.float32) - SUB // 2) / SUB
    live_mask = jnp.where(jnp.arange(VIS)[None, :] < counts[:, None], 1.0 / math.sqrt(VIS), 0.0)
    vis_real = samples[:, 0] * live_mask
    vis_imag = samples[:, 1] * live_mask
    angle_u = 2.0 * math.pi * samples[:, 2, :, None] * position
    angle_v = 2.0 * math.pi * samples[:, 3, :, None] * position
    cos_u, sin_u = (jnp.cos(angle_u), jnp.sin(angle_u))
    cos_v, sin_v = (jnp.cos(angle_v), jnp.sin(angle_v))
    table_real, table_imag = dft_table(SUB, 1.0 / math.sqrt(SUB))
    weight_real = vis_real[:, :, None] * cos_u - vis_imag[:, :, None] * sin_u
    weight_imag = vis_real[:, :, None] * sin_u + vis_imag[:, :, None] * cos_u
    pixel_real, pixel_imag = cplx_einsum("nki,nkj->nij", weight_real, weight_imag, cos_v, sin_v)
    half_real, half_imag = cplx_einsum(
        "nij,ip->npj", pixel_real, pixel_imag, table_real, table_imag
    )
    spec_real, spec_imag = cplx_einsum("npj,jq->npq", half_real, half_imag, table_real, table_imag)
    return jnp.stack([spec_real, spec_imag], axis=1).reshape(subgrid_count, 2 * SUB * SUB)


def transform_last(real_x, imag_x):
    row_count = real_x.shape[0]
    outer_size = GRID // FA
    outer_real, outer_imag = dft_table(outer_size, 1.0 / math.sqrt(outer_size))
    inner_real, inner_imag = dft_table(FA, 1.0 / math.sqrt(FA))
    twist_real, twist_imag = twiddle_table()
    first_real, first_imag = cplx_einsum(
        "rqn,qk->rkn",
        real_x.reshape(row_count, outer_size, FA),
        imag_x.reshape(row_count, outer_size, FA),
        outer_real,
        outer_imag,
    )
    turned_real = first_real * twist_real - first_imag * twist_imag
    turned_imag = first_real * twist_imag + first_imag * twist_real
    final_real, final_imag = cplx_einsum(
        "rkn,nm->rmk", turned_real, turned_imag, inner_real, inner_imag
    )
    return (final_real.reshape(row_count, GRID), final_imag.reshape(row_count, GRID))


def transform_first(real_x, imag_x):
    col_count = real_x.shape[1]
    outer_size = GRID // FA
    outer_real, outer_imag = dft_table(outer_size, 1.0 / math.sqrt(outer_size))
    inner_real, inner_imag = dft_table(FA, 1.0 / math.sqrt(FA))
    twist_real, twist_imag = twiddle_table()
    first_real, first_imag = cplx_einsum(
        "qnc,qk->knc",
        real_x.reshape(outer_size, FA, col_count),
        imag_x.reshape(outer_size, FA, col_count),
        outer_real,
        outer_imag,
    )
    turned_real = first_real * twist_real[:, :, None] - first_imag * twist_imag[:, :, None]
    turned_imag = first_real * twist_imag[:, :, None] + first_imag * twist_real[:, :, None]
    final_real, final_imag = cplx_einsum(
        "knc,nm->mkc", turned_real, turned_imag, inner_real, inner_imag
    )
    return (final_real.reshape(GRID, col_count), final_imag.reshape(GRID, col_count))


def per_device(visibilities, offsets, vis_count, owner, tile_row, tile_col):
    owners = lax.axis_size("wide")
    capacity = 3 * SUB_DEV // owners
    band_tiles = GRID // (SUB * owners)
    tile_cols = GRID // SUB
    spectrum_size = 2 * SUB * SUB
    samples = jnp.concatenate([visibilities, offsets], axis=1)
    tile_ids = (tile_row * tile_cols + tile_col).astype(jnp.float32)
    onehot = (owner[:, None] == jnp.arange(owners)[None, :]).astype(jnp.int32)
    ranked = jnp.cumsum(onehot, axis=0) - 1
    slot_of = jnp.sum(ranked * onehot, axis=1)
    local_spectra = subgrid_spectra(samples, vis_count.astype(jnp.float32))
    packed = (
        jnp.zeros((owners, capacity, spectrum_size), jnp.float32)
        .at[owner, slot_of]
        .set(local_spectra)
    )
    labels = jnp.zeros((owners, capacity), jnp.float32).at[owner, slot_of].set(tile_ids)
    got_spectra, got_ids = (
        lax.all_to_all(packed, "wide", split_axis=0, concat_axis=0, tiled=True),
        lax.all_to_all(labels, "wide", split_axis=0, concat_axis=0, tiled=True),
    )
    received = got_spectra.reshape(-1, spectrum_size)
    tile_index = got_ids.reshape(-1).astype(jnp.int32)
    grid_tiles = (
        jnp.zeros((band_tiles * tile_cols, spectrum_size), jnp.float32).at[tile_index].add(received)
    )
    grid_band = grid_tiles.reshape(band_tiles, tile_cols, 2, SUB, SUB).transpose(2, 0, 3, 1, 4)
    grid_band = grid_band.reshape(2, band_tiles * SUB, GRID)
    row_real, row_imag = transform_last(grid_band[0], grid_band[1])
    column_band = lax.all_to_all(
        jnp.stack([row_real, row_imag]), "wide", split_axis=2, concat_axis=1, tiled=True
    )
    out_real, out_imag = transform_first(column_band[0], column_band[1])
    return jnp.stack([out_real, out_imag])


def solution(mesh):
    placed = (
        P(("group", "wide"), None, None),
        P(("group", "wide"), None, None),
        P(("group", "wide")),
        P(("group", "wide")),
        P(("group", "wide")),
        P(("group", "wide")),
    )
    return jax.shard_map(
        per_device, mesh=mesh, in_specs=placed, out_specs=P(None, "group", "wide"), check_vma=False
    )
```

profile of v0, /device:TPU:15, one launch (start us, length us, event | category | flops | bytes accessed | tf_op | source)
XLA Modules:
  0.0 782.8 jit_solution(1957485155887494097)
XLA Ops:
  0.7 0.7 iota_compare_fusion
  2.3 0.7 fusion.129
  3.0 0.7 add_convert_fusion
  4.3 27.3 %scatter_fusion = f32[16,36]{1,0:T(8,128)} fusion(f32[16,36]{1,0:T(8,128)} %broadcast_in_dim.17, s32[192]{0:T(256)S(1)} %bitcast.127, f32[192]{0:T(256)S(1)} %add_convert_fusion), kind=kCustom, calls=%fused_computation | custom fusion | bytes 3840 | tf_op jit(solution)/shard_map/scatter | solution.py:123
  31.6 6.5 all-to-all-start
  38.8 1.2 fusion.282
  40.0 1.3 slice_multiply_fusion.1
  41.4 28.1 %fusion.4 = f32[192,32,32]{2,1,0:T(8,128)} fusion(f32[192,128]{1,0:T(8,128)S(1)} %bitcast.147, f32[192,128]{1,0:T(8,128)S(1)} %get-tuple-element.18, f32[32]{0:T(128)S(1)} %add_multiply_fusion, f32[192,128]{1,0:T(8,128)S(1)} %bitcast.143, f32[192,128]{1,0:T(8,128)S(1)} %get-tuple-element.17), kind=kOutput, calls=%fused_computation.13 | convolution fusion | flops 305922048 | bytes 1179776 | tf_op jit(solution)/shard_map/nki,nkj->nij/dot_general | solution.py:21
  69.5 27.0 %fusion.5 = f32[192,32,32]{2,1,0:T(8,128)S(1)} fusion(f32[192,128]{1,0:T(8,128)S(1)} %bitcast.148, f32[192,128]{1,0:T(8,128)S(1)} %get-tuple-element.18, f32[32]{0:T(128)S(1)} %add_multiply_fusion, f32[192,128]{1,0:T(8,128)S(1)} %bitcast.144, f32[192,128]{1,0:T(8,128)S(1)} %get-tuple-element.17), kind=kOutput, calls=%fused_computation.14 | convolution fusion | flops 305922048 | bytes 1179776 | tf_op jit(solution)/shard_map/nki,nkj->nij/dot_general | solution.py:21
  96.5 28.3 %fusion.56 = f32[192,32,32]{2,1,0:T(8,128)} fusion(f32[192,32,32]{2,1,0:T(8,128)S(1)} %fusion.5, f32[192,128]{1,0:T(8,128)S(1)} %bitcast.149, f32[192,128]{1,0:T(8,128)S(1)} %get-tuple-element.18, f32[32]{0:T(128)S(1)} %add_multiply_fusion, f32[192,128]{1,0:T(8,128)S(1)} %bitcast.145, f32[192,128]{1,0:T(8,128)S(1)} %get-tuple-element.17), kind=kOutput, calls=%fused_computation.58 | convolution fusion | flops 306118656 | bytes 1966208 | tf_op jit(solution)/shard_map/nki,nkj->nij/dot_general | solution.py:21
  124.8 3.4 copy.136
  128.2 1.1 fusion.137
  129.3 1.1 fusion.148
  130.4 28.3 %fusion.59 = f32[192,32,32]{2,1,0:T(8,128)} fusion(f32[192,32,32]{2,1,0:T(8,128)S(1)} %copy-done.7, f32[192,128]{1,0:T(8,128)S(1)} %bitcast.150, f32[192,128]{1,0:T(8,128)S(1)} %get-tuple-element.18, f32[32]{0:T(128)S(1)} %add_multiply_fusion, f32[192,128]{1,0:T(8,128)S(1)} %bitcast.146, f32[192,128]{1,0:T(8,128)S(1)} %get-tuple-element.17), kind=kOutput, calls=%fused_computation.59 | convolution fusion | flops 306118656 | bytes 1966208 | tf_op jit(solution)/shard_map/nki,nkj->nij/dot_general | solution.py:21
  158.7 3.5 copy.137
  162.2 1.1 fusion.85
  163.3 1.7 fusion.88
  165.0 1.7 fusion.90
  166.8 1.1 fusion.84
  167.9 1.7 fusion.83
  169.6 1.7 fusion.82
  171.6 1.7 copy.144
  173.3 2.7 broadcast_in_dim.19
  176.0 34.4 %scatter_fusion.1 = f32[16,36,2048]{2,0,1:T(8,128)} fusion(f32[16,36,2048]{2,0,1:T(8,128)} %broadcast_in_dim.19, s32[192]{0:T(256)S(1)} %bitcast.128, f32[192,2048]{1,0:T(8,128)S(1)} %copy-done.6), kind=kCustom, calls=%fused_computation.1 | custom fusion | bytes 4720128 | tf_op jit(solution)/shard_map/scatter | solution.py:121
  210.4 7.5 copy.145
  217.8 6.1 all-to-all-start.1
  224.2 114.7 %all-to-all-done.1 = f32[16,36,2048]{2,1,0:T(8,128)} async-done(((f32[16,36,2048]{2,1,0:T(8,128)}), f32[16,36,2048]{2,1,0:T(8,128)}, u32[]{:S(2)}, u32[]{:S(2)}) %all-to-all-start.1) | async-done | bytes 4718624 | tf_op jit(solution)/shard_map/all_to_all | solution.py:125
  338.9 5.3 reshape.253
  344.2 18.6 %scatter_custom_fusion.2 = f32[1024,2048]{1,0:T(8,128)} fusion(s32[576]{0:T(1024)S(1)} %fusion.158, f32[576,2048]{1,0:T(8,128)} %reshape.253, f32[]{:T(128)} %constant.88.clone.1), kind=kCustom, calls=%fused_computation.23 | custom fusion | flops 1179648 | bytes 8389120 | tf_op jit(solution)/shard_map/scatter-add | solution.py:131
  362.8 9.7 %copy.146 = f32[1024,2048]{0,1:T(8,128)} copy(f32[1024,2048]{1,0:T(8,128)} %scatter_custom_fusion.2) | data formatting | bytes 16777216 | tf_op jit(solution)/shard_map/scatter-add | solution.py:131
  372.4 5.5 copy.174
  377.9 3.8 fusion.281
  381.8 10.5 %copy.147 = f32[1,8,32,128,32]{4,3,2,1,0:T(8,128)} copy(f32[1,8,32,128,32]{3,1,4,2,0:T(8,128)} %get-tuple-element.12) | data formatting | bytes 8388608 | tf_op jit(solution)/shard_map/slice | solution.py:135
  392.2 12.0 %reshape_squeeze.12 = f32[256,32,128]{2,1,0:T(8,128)} reshape(f32[1,8,32,128,32]{4,3,2,1,0:T(8,128)} %copy.147) | data formatting | bytes 8388608 | tf_op jit(solution)/shard_map/reshape;squeeze | solution.py:72
  404.2 8.0 %fusion.132 = f32[32,256,128]{2,0,1:T(8,128)} fusion(f32[256,32,128]{2,1,0:T(8,128)} %reshape_squeeze.12), kind=kOutput, calls=%fused_computation.145 | convolution fusion | flops 402668544 | bytes 8388608 | tf_op jit(solution)/shard_map/rqn,qk->rkn/dot_general | solution.py:21
  412.2 5.2 fusion.143
  417.4 10.5 %copy.148 = f32[1,8,32,128,32]{4,3,2,1,0:T(8,128)} copy(f32[1,8,32,128,32]{3,1,4,2,0:T(8,128)} %get-tuple-element.11) | data formatting | bytes 8388608 | tf_op jit(solution)/shard_map/slice | solution.py:135
  427.8 12.1 %reshape_squeeze.13 = f32[256,32,128]{2,1,0:T(8,128)} reshape(f32[1,8,32,128,32]{4,3,2,1,0:T(8,128)} %copy.148) | data formatting | bytes 8388608 | tf_op jit(solution)/shard_map/reshape;squeeze | solution.py:73
  440.0 7.9 %convolution_add_fusion = f32[32,256,128]{2,0,1:T(8,128)S(1)} fusion(f32[32,256,128]{2,0,1:T(8,128)} %fusion.132, f32[256,32,128]{2,1,0:T(8,128)} %reshape_squeeze.13), kind=kOutput, calls=%fused_computation.55 | convolution fusion | flops 403717120 | bytes 12582912 | tf_op jit(solution)/shard_map/rqn,qk->rkn/dot_general | solution.py:21
  447.9 5.1 subtract_bitcast_fusion.1
  453.0 6.5 fusion.26
  459.5 6.2 fusion.28
  465.7 6.6 subtract_bitcast_fusion
  472.3 6.2 add_bitcast_fusion
  478.5 2.4 copy.154
  481.0 2.6 copy.151
  484.1 23.4 %copy.155 = f32[2,256,4096]{1,0,2:T(2,128)} copy(f32[2,256,4096]{1,2,0:T(8,128)S(1)} %pad_maximum_fusion) | data formatting | bytes 16777216 | tf_op jit(solution)/shard_map/stack | solution.py:137
  507.6 4.8 all-to-all-start.2
  512.6 182.2 %all-to-all-done.2 = f32[2,256,4096]{1,0,2:T(2,128)} async-done(((f32[2,256,4096]{1,0,2:T(2,128)}), f32[2,256,4096]{1,0,2:T(2,128)}, u32[]{:S(2)}, u32[]{:S(2)}) %all-to-all-start.2) | async-done | bytes 8388640 | tf_op jit(solution)/shard_map/all_to_all | solution.py:136
  694.7 4.0 copy.156
  698.8 3.9 fusion.280
  702.6 5.3 copy.159
  708.0 10.1 %fusion.18 = f32[32,128,256]{2,0,1:T(8,128)} fusion(f32[32,128,256]{2,1,0:T(8,128)} %bitcast.131), kind=kOutput, calls=%fused_computation.33 | convolution fusion | flops 402668544 | bytes 8388608 | tf_op jit(solution)/shard_map/qnc,qk->knc/dot_general | solution.py:21
  718.1 7.0 fusion.20
  725.1 5.7 copy.157
  730.8 10.0 %fusion.44 = f32[32,128,256]{2,0,1:T(8,128)S(1)} fusion(f32[32,128,256]{2,0,1:T(8,128)} %fusion.20, f32[32,128,256]{2,1,0:T(8,128)} %bitcast.129), kind=kOutput, calls=%fused_computation.51 | convolution fusion | flops 403717120 | bytes 12582912 | tf_op jit(solution)/shard_map/qnc,qk->knc/dot_general | solution.py:21
  740.8 7.8 %multiply_subtract_fusion = (f32[32,128,256]{2,0,1:T(8,128)S(1)}, f32[32,128,256]{2,0,1:T(8,128)S(1)}) fusion(f32[32,128,256]{2,0,1:T(8,128)S(1)} %fusion.44, f32[32,128]{0,1:T(8,128)S(1)} %copy.164, f32[32,128]{0,1:T(8,128)S(1)} %copy.161, f32[32,128,256]{2,0,1:T(8,128)S(1)} %copy-done.5, f32[32,128,256]{2,1,0:T(8,128)S(1)} %bitcast.130), kind=kOutput, calls=%fused_computation.18 | convolution fusion | flops 410008576 | bytes 21004288 | tf_op jit(solution)/shard_map/qnc,qk->knc/dot_general | solution.py:21
  748.7 6.2 fusion.10
  754.9 6.2 fusion.12
  761.1 6.0 fusion.50
  767.2 6.4 fusion.53
  773.6 2.4 copy.170
  776.0 2.4 copy.167
  778.4 3.9 pad_maximum_fusion.1
  (38 shorter events, 4.2 us)
Async XLA Ops:
  31.6 186.3 %all-to-all-start = ((f32[16,1,36]{2,1,0:T(1,128)}), f32[16,1,36]{2,1,0:T(1,128)S(1)}, u32[]{:S(2)}, u32[]{:S(2)}) async-start(f32[16,1,36]{2,1,0:T(1,128)} %bitcast.7), calls=%async_computation | async-start | bytes 16384 | tf_op jit(solution)/shard_map/all_to_all | solution.py:126
  128.2 2.2 copy-start.7
  173.3 2.7 copy-start.6
  217.8 121.1 %all-to-all-start.1 = ((f32[16,36,2048]{2,1,0:T(8,128)}), f32[16,36,2048]{2,1,0:T(8,128)}, u32[]{:S(2)}, u32[]{:S(2)}) async-start(f32[16,36,2048]{2,1,0:T(8,128)} %copy.145), calls=%async_computation.1 | async-start | bytes 10485760 | tf_op jit(solution)/shard_map/all_to_all | solution.py:125
  404.2 8.0 %copy-start.2 = (f32[256,32,128]{2,1,0:T(8,128)S(1)}, f32[256,32,128]{2,1,0:T(8,128)}, u32[]{:S(2)}) copy-start(f32[256,32,128]{2,1,0:T(8,128)} %reshape_squeeze.12) | copy-start | bytes 12582916
  440.0 8.0 %copy-start = (f32[256,32,128]{2,1,0:T(8,128)S(1)}, f32[256,32,128]{2,1,0:T(8,128)}, u32[]{:S(2)}) copy-start(f32[256,32,128]{2,1,0:T(8,128)} %reshape_squeeze.13) | copy-start | bytes 12582916
  440.0 8.0 %copy-start.4 = (f32[32,256,128]{2,0,1:T(8,128)S(1)}, f32[32,256,128]{2,0,1:T(8,128)}, u32[]{:S(2)}) copy-start(f32[32,256,128]{2,0,1:T(8,128)} %fusion.143) | copy-start | bytes 12582916
  507.6 187.1 %all-to-all-start.2 = ((f32[2,256,4096]{1,0,2:T(2,128)}), f32[2,256,4096]{1,0,2:T(2,128)}, u32[]{:S(2)}, u32[]{:S(2)}) async-start(f32[2,256,4096]{1,0,2:T(2,128)} %copy.155), calls=%async_computation.2 | async-start | bytes 16777216 | tf_op jit(solution)/shard_map/all_to_all | solution.py:136
  708.0 10.1 %copy-start.3 = (f32[1,16,256,256]{3,2,1,0:T(8,128)S(1)}, f32[1,16,256,256]{3,2,1,0:T(8,128)}, u32[]{:S(2)}) copy-start(f32[1,16,256,256]{3,2,1,0:T(8,128)} %copy.159) | copy-start | bytes 12582916
  730.8 10.0 %copy-start.1 = (f32[1,16,256,256]{3,2,1,0:T(8,128)S(1)}, f32[1,16,256,256]{3,2,1,0:T(8,128)}, u32[]{:S(2)}) copy-start(f32[1,16,256,256]{3,2,1,0:T(8,128)} %copy.157) | copy-start | bytes 12582916
  730.8 10.0 %copy-start.5 = (f32[32,128,256]{2,0,1:T(8,128)S(1)}, f32[32,128,256]{2,0,1:T(8,128)}, u32[]{:S(2)}) copy-start(f32[32,128,256]{2,0,1:T(8,128)} %fusion.18) | copy-start | bytes 12582916
where the time goes:
time: 791 us; the launch traced here: 783 us
  waiting for transfers between devices  297 us (38%)
  matrix products  234 us (30%)
  local copies, waits for them, and re-layouts  204 us (26%)
  other arithmetic  29 us (4%)
  starting transfers between devices  17.5 us (2%)
    dot_general x28, matrix products, single(): return jnp.einsum(pattern, first, second, precision=highest)  234 us
    all_to_all x1, waiting for transfers between devices, per_device(): lax.all_to_all(jnp.stack([row_real, row_imag]), 'wide', split_axis=2, con...  182 us
    all_to_all x1, waiting for transfers between devices, per_device(): lax.all_to_all(packed, 'wide', split_axis=0, concat_axis=0, tiled=True)  115 us
    scatter x2, local copies, waits for them, and re-layouts, per_device(): packed = jnp.zeros((owners, capacity, spectrum_size), jnp.float32).at[own...  41.9 us
    scatter x1, local copies, waits for them, and re-layouts, per_device(): jnp.zeros((owners, capacity), jnp.float32).at[owner, slot_of].set(tile_ids)  27.3 us
    slice x3, local copies, waits for them, and re-layouts, per_device(): row_real, row_imag = transform_last(grid_band[0], grid_band[1])  24.8 us
    another operation x1, local copies, waits for them, and re-layouts, per_device(): jnp.stack([row_real, row_imag])  23.4 us
    scatter-add x1, other arithmetic, per_device(): jnp.zeros((band_tiles * tile_cols, spectrum_size), jnp.float32)  18.6 us
  transfers between devices with their start and end apart: 3, of which 2 were waited for; matrix products, arithmetic and copies ran while one was open for 23% of the time, Pallas kernels for 0%

commit v1 on v0

v1 whole, which is shorter than its diff:
```python
import functools
import math

import jax
import jax.numpy as jnp
import numpy as np
from jax import lax
from jax.experimental import pallas as pl
from jax.experimental.pallas import tpu as pltpu
from jax.sharding import PartitionSpec as P

SUB = 32
VIS = 128
GRID = 4096
TILES = GRID // SUB
F32 = jnp.float32
BF16 = jnp.bfloat16


def _poly_coefs():
    nodes = 0.125 * (1 + np.cos(np.pi * (np.arange(64) + 0.5) / 64))
    r = np.sqrt(nodes)
    cheb = np.polynomial.chebyshev.Chebyshev
    c = cheb.fit(nodes, np.cos(2 * np.pi * r), 5, domain=[0, 0.25])
    s = cheb.fit(nodes, np.sin(2 * np.pi * r) / r, 5, domain=[0, 0.25])
    poly = np.polynomial.Polynomial
    return (
        [float(v) for v in c.convert(kind=poly).coef],
        [float(v) for v in s.convert(kind=poly).coef],
    )


COS_C, SIN_C = _poly_coefs()


def cis(turns):
    r = turns - jnp.round(turns)
    z = r * r
    c = COS_C[5]
    s = SIN_C[5]
    for k in range(4, -1, -1):
        c = c * z + COS_C[k]
        s = s * z + SIN_C[k]
    return c, s * r


def split(x):
    hi = x.astype(BF16)
    lo = (x - hi.astype(F32)).astype(BF16)
    return hi, lo


def np_tables():
    t = np.arange(SUB)
    q = np.arange(SUB)
    n0 = np.arange(TILES)
    g = np.einsum(
        "tq,qn->tn",
        np.exp(-2j * np.pi * np.outer(t, q) / SUB),
        np.exp(-2j * np.pi * np.outer(q, n0) / GRID),
    )
    w = np.exp(-2j * np.pi * (np.outer(n0, n0) % TILES) / TILES)
    return g, w


def pixel_kernel(block, ar_ref, ai_ref, u_ref, v_ref, out_ref):
    row8 = lax.broadcasted_iota(jnp.int32, (8, VIS), 0)
    step = row8.astype(F32) / SUB
    low = row8 < 4
    coarse = ((row8 & 3) * 8 - 16).astype(F32) / SUB
    lane = lax.broadcasted_iota(jnp.int32, (16, VIS), 1)

    def bc(ref, s):
        return jnp.broadcast_to(ref[pl.ds(s, 1), :], (8, VIS))

    def one(s):
        u, v, ar, ai = bc(u_ref, s), bc(v_ref, s), bc(ar_ref, s), bc(ai_ref, s)
        eur, eui = cis(u * step)
        evr, evi = cis(v * step)
        fr, fi = cis(jnp.where(low, u, v) * coarse)
        wr, wi = ar * fr - ai * fi, ar * fi + ai * fr
        pieces = [[], [], [], []]
        for a in range(4):
            gr = jnp.broadcast_to(wr[a : a + 1], (8, VIS))
            gi = jnp.broadcast_to(wi[a : a + 1], (8, VIS))
            hr = jnp.broadcast_to(fr[4 + a : 5 + a], (8, VIS))
            hi = jnp.broadcast_to(fi[4 + a : 5 + a], (8, VIS))
            pieces[0].append(eur * gr - eui * gi)
            pieces[1].append(eur * gi + eui * gr)
            pieces[2].append(evr * hr - evi * hi)
            pieces[3].append(evr * hi + evi * hr)
        tw_r, tw_i, tv_r, tv_i = (jnp.concatenate(p, axis=0) for p in pieces)
        wrh, wrl = split(tw_r)
        wih, wil = split(tw_i)
        vrh, vrl = split(tv_r)
        vih, vil = split(tv_i)
        cat = jnp.concatenate
        lhs = cat([cat([wrh, wih], 1), cat([wrl, wil], 1)], 0)
        rhs = cat(
            [
                cat([vrh, -vih], 1),
                cat([vih, vrh], 1),
                cat([vrl, -vil], 1),
                cat([vil, vrl], 1),
            ],
            0,
        )
        prod = lax.dot_general(
            lhs, rhs, (((1,), (1,)), ((), ())), preferred_element_type=F32
        )
        q = prod[:32] + prod[32:]
        q = q + pltpu.roll(q, 64, 1)
        out_ref[s] = jnp.where(lane < 64, q[:16], q[16:])

    def body(t, carry):
        for d in range(4):
            one(t * 4 + d)
        return carry

    lax.fori_loop(0, block // 4, body, 0)


def pixels(ar, ai, u, v, block):
    count = ar.shape[0]
    spec = pl.BlockSpec((block, VIS), lambda g: (g, 0))
    return pl.pallas_call(
        functools.partial(pixel_kernel, block),
        out_shape=jax.ShapeDtypeStruct((count, 16, 128), F32),
        grid=(count // block,),
        in_specs=[spec] * 4,
        out_specs=pl.BlockSpec((block, 16, 128), lambda g: (g, 0, 0)),
        name="pixels",
    )(ar, ai, u, v)


def spread_kernel(block, nc, r_ref, c_ref, p_ref, phr_ref, phi_ref, tab_ref, x_ref, y_ref):
    g = pl.program_id(0)
    halves = nc // 128
    chunk = 8
    rows = chunk * 16

    @pl.when(g == 0)
    def _():
        def zero(t, carry):
            x_ref[t] = jnp.zeros(x_ref.shape[1:], F32)
            return carry

        lax.fori_loop(0, TILES, zero, 0)

    lane = lax.broadcasted_iota(jnp.int32, (rows, 128), 1)

    def multiply(t, slot):
        p = p_ref[pl.ds(t * chunk, chunk)].reshape(rows, 128)
        hi = p.astype(BF16)
        hif = hi.astype(F32)
        lof = p - hif
        hir = pltpu.roll(hif, 64, 1)
        lor = pltpu.roll(lof, 64, 1)
        first = jnp.where(lane < 64, hif, lor).astype(BF16)
        second = jnp.where(lane < 64, hir, lof).astype(BF16)
        lhs = jnp.concatenate(
            [
                jnp.concatenate([first, hi], 1),
                jnp.concatenate([second, hir.astype(BF16)], 1),
            ],
            0,
        )
        y_ref[slot] = jnp.dot(lhs, tab_ref[...], preferred_element_type=F32)

    def add(t, slot):
        for d in range(chunk):
            s = g * block + t * chunk + d
            r = r_ref[s]
            c = c_ref[s]
            pr = phr_ref[c]
            pi = phi_ref[c]
            for half in range(2):
                for sub in range(2):
                    src = half * rows + d * 16 + sub * 8
                    dst = half * 16 + sub * 8
                    for n in range(halves):
                        re = pl.ds(n * 128, 128)
                        im = pl.ds(nc + n * 128, 128)
                        yr = y_ref[slot, pl.ds(src, 8), re]
                        yi = y_ref[slot, pl.ds(src, 8), im]
                        x_ref[r, pl.ds(dst, 8), re] += yr * pr - yi * pi
                        x_ref[r, pl.ds(dst, 8), im] += yr * pi + yi * pr

    steps = block // chunk
    multiply(0, 0)

    def body(t, carry):
        multiply(2 * t + 1, 1)
        add(2 * t, 0)
        multiply(2 * t + 2, 0)
        add(2 * t + 1, 1)
        return carry

    lax.fori_loop(0, steps // 2 - 1, body, 0)
    multiply(steps - 1, 1)
    add(steps - 2, 0)
    add(steps - 1, 1)


def spread(rows, cols, pix, phr, phi, table, nc, block):
    count = pix.shape[0]
    const = lambda shape: pl.BlockSpec(shape, lambda g, r, c: (0,) * len(shape))
    return pl.pallas_call(
        functools.partial(spread_kernel, block, nc),
        out_shape=jax.ShapeDtypeStruct((TILES, SUB, 2 * nc), F32),
        grid_spec=pltpu.PrefetchScalarGridSpec(
            num_scalar_prefetch=2,
            grid=(count // block,),
            in_specs=[
                pl.BlockSpec((block, 16, 128), lambda g, r, c: (g, 0, 0)),
                const((TILES, 8, 128)),
                const((TILES, 8, 128)),
                const((256, 2 * nc)),
            ],
            out_specs=const((TILES, SUB, 2 * nc)),
            scratch_shapes=[pltpu.VMEM((2, 256, 2 * nc), F32)],
        ),
        name="spread",
    )(rows, cols, pix, phr, phi, table)


def np_split(x):
    hi = x.astype(np.float32).astype(BF16)
    return hi, (x - hi.astype(np.float64)).astype(BF16)


def column_table(g, nc):
    first = lax.axis_index("wide") * (nc // 128)
    doubled = np.concatenate([g, g]) / 512.0

    def take(values):
        picked = [
            lax.dynamic_slice(jnp.asarray(values), (first + n, 0), (SUB, 128))
            for n in range(nc // 128)
        ]
        return jnp.concatenate(picked, 1)

    def full(dr, di):
        dr, di = take(dr), take(di)
        return jnp.concatenate(
            [jnp.concatenate([dr, di], 1), jnp.concatenate([-di, dr], 1)], 0
        )

    rh, rl = np_split(doubled.real)
    ih, il = np_split(doubled.imag)
    hi, lo = full(rh, ih), full(rl, il)
    return jnp.concatenate([hi, hi, lo, jnp.zeros_like(hi)], 0)


def real_form(z):
    return np.array([[z.real, -z.imag], [z.imag, z.real]])


def per_device(visibilities, offsets, vis_count, owner, tile_row, tile_col):
    wide = lax.axis_size("wide")
    nc = GRID // wide
    band = GRID // (SUB * wide)
    g, w = np_tables()
    live = jnp.where(
        jnp.arange(VIS)[None, :] < vis_count[:, None], 1.0 / math.sqrt(VIS), 0.0
    )
    tile = (owner * band + tile_row) * TILES + tile_col
    tile = lax.all_gather(tile, "wide", tiled=True)
    pix = pixels(
        visibilities[:, 0] * live,
        visibilities[:, 1] * live,
        offsets[:, 0],
        offsets[:, 1],
        64,
    )
    pix = lax.all_gather(pix, "wide", tiled=True)
    spread8 = lambda m: jnp.broadcast_to(jnp.asarray(m, F32)[:, None, :], (TILES, 8, 128))
    x = spread(
        tile // TILES,
        tile % TILES,
        pix,
        spread8(w.real),
        spread8(w.imag),
        column_table(g, nc),
        nc,
        64,
    )
    x = x.reshape(TILES, SUB, 2, nc)
    c4 = jnp.asarray(real_form(w).transpose(0, 2, 1, 3), F32)
    z = jnp.einsum("omcr,ricn->moin", c4, x, precision=lax.Precision.HIGH)
    index = (np.arange(SUB)[:, None] + np.arange(SUB)[None, :]) % SUB
    m4 = real_form(g[index] / 256.0)
    m4 = jnp.asarray(m4.transpose(4, 0, 3, 1, 2), F32)
    out = jnp.einsum("mpkoi,moin->pkmn", m4, z, precision=lax.Precision.HIGH)
    return out.reshape(2, GRID, nc)


def solution(mesh):
    placed = (
        P(("group", "wide"), None, None),
        P(("group", "wide"), None, None),
        P(("group", "wide")),
        P(("group", "wide")),
        P(("group", "wide")),
        P(("group", "wide")),
    )
    return jax.shard_map(
        per_device, mesh=mesh, in_specs=placed, out_specs=P(None, "group", "wide"), check_vma=False
    )
```

time: 791 us -> 302 us (0.38)
  waiting for transfers between devices: 297 us -> 78.6 us
  matrix products: 234 us -> 16.4 us
  local copies, waits for them, and re-layouts: 204 us -> 38.1 us
  Pallas kernels: 0 us -> 102 us
  blocking collectives: 0 us -> 46.7 us
  other arithmetic: 29 us -> 3.01 us
  starting transfers between devices: 17.5 us -> 0.01 us
  between operations: 0.84 us -> 14.2 us
    all_to_all x3 -> x0, waiting for transfers between devices: 297 us -> none  [the longest x1 182 us: per_device(): lax.all_to_all(jnp.stack([row_real, row_imag]), 'wide', split_axis=2, con...]
    dot_general x28 -> x2, matrix products: 234 us -> 16.4 us  [the longest x1 8.49 us: per_device(): out = jnp.einsum('mpkoi,moin->pkmn', m4, z, precision=lax.Precision.HIGH)]
    pallas_call x0 -> x2, Pallas kernels: none -> 102 us  [the longest x1 85.8 us: spread(): pl.pallas_call(functools.partial(spread_kernel, block, nc), out_shape=jax...]
    all_gather x0 -> x1, waiting for transfers between devices: none -> 78.6 us  [per_device(): pix = lax.all_gather(pix, 'wide', tiled=True)]
    scatter x3 -> x0, local copies, waits for them, and re-layouts: 69.1 us -> none  [the longest x2 41.9 us: per_device(): packed = jnp.zeros((owners, capacity, spectrum_size), jnp.float32).at[own...]
    another operation x4 -> x0, local copies, waits for them, and re-layouts: 47.5 us -> none  [the longest x1 23.4 us: per_device(): jnp.stack([row_real, row_imag])]
    unnamed x0 -> x1, blocking collectives: none -> 46.7 us
    slice x8 -> x2, local copies, waits for them, and re-layouts: 41.1 us -> 3.06 us  [the longest x1 1.87 us: per_device(): offsets[:, 1]]
  transfers between devices with their start and end apart: 3 -> 1, of which waited for: 2 -> 1; matrix products, arithmetic and copies ran while one was open for 23% -> 1% of each run, Pallas kernels for 0% -> 0%
where the time goes in v1:
time: 302 us; the launch traced here: 299 us
  Pallas kernels  102 us (34%)
  waiting for transfers between devices  78.6 us (26%)
  blocking collectives  46.7 us (15%)
  local copies, waits for them, and re-layouts  38.1 us (13%)
  matrix products  16.4 us (5%)
  between operations  14.2 us (5%)
    pallas_call x1, Pallas kernels, spread(): pl.pallas_call(functools.partial(spread_kernel, block, nc), out_shape=jax...  85.8 us
    all_gather x1, waiting for transfers between devices, per_device(): pix = lax.all_gather(pix, 'wide', tiled=True)  78.6 us
    unnamed x1, blocking collectives  46.7 us
    pallas_call x1, Pallas kernels, pixels(): pl.pallas_call(functools.partial(pixel_kernel, block), out_shape=jax.Shap...  16.6 us
    transpose x1, local copies, waits for them, and re-layouts, per_device(): z = jnp.einsum('omcr,ricn->moin', c4, x, precision=lax.Precision.HIGH)  10.3 us
    reshape x1, local copies, waits for them, and re-layouts, per_device(): x = x.reshape(TILES, SUB, 2, nc)  10.1 us
    dot_general x1, matrix products, per_device(): out = jnp.einsum('mpkoi,moin->pkmn', m4, z, precision=lax.Precision.HIGH)  8.49 us
    transpose x1, local copies, waits for them, and re-layouts, per_device(): out = jnp.einsum('mpkoi,moin->pkmn', m4, z, precision=lax.Precision.HIGH)  8.25 us
  transfers between devices with their start and end apart: 1, of which 1 were waited for; matrix products, arithmetic and copies ran while one was open for 1% of the time, Pallas kernels for 0%

profile of v1, /device:TPU:15, one launch (start us, length us, event | category | flops | bytes accessed | tf_op | source)
XLA Modules:
  0.0 299.4 jit_solution(3720390945835297545)
XLA Ops:
  6.5 0.0 all-gather.2.cloned.1.call-start
  6.5 1.2 fusion.3
  7.7 1.9 fusion.2
  9.6 1.4 select_multiply_fusion
  11.0 16.6 %pixels.1 = f32[192,16,128]{2,1,0:T(8,128)} custom-call(f32[192,128]{1,0:T(8,128)} %get-tuple-element.20.ar_ref, f32[192,128]{1,0:T(8,128)} %get-tuple-element.19.ai_ref, f32[192,128]{1,0:T(8,128)} %bitcast.40, f32[192,128]{1,0:T(8,128)} %bitcast.39), custom_call_target="tpu_custom_call" | custom-call | tf_op jit(solution)/shard_map/pixels/pallas_call | solution.py:126
  27.6 0.0 all-gather.2.cloned.1.call-update
  27.7 1.3 dynamic-slice
  29.7 0.8 add_dynamic-update-slice_fusion
  30.5 46.7 %all-reduce = s32[3072]{0:T(1024)S(1)} all-reduce(s32[3072]{0:T(1024)S(1)} %add_dynamic-update-slice_fusion), channel_id=1, replica_groups=mesh['group'=2,'wide'=16] {'wide'}, use_global_device_ids=true, to_apply=%add | all-reduce | flops 3072 | bytes 24576
  77.2 0.8 constant_dynamic-slice_fusion.5
  78.0 0.8 constant_dynamic-slice_fusion.1
  78.9 0.0 copy-start
  79.0 0.7 add_select_fusion
  79.6 78.6 %all-gather.2.cloned.1.call-done.p_ref = f32[3072,16,128]{2,1,0:T(8,128)} async-done(((f32[192,16,128]{2,1,0:T(8,128)}), f32[3072,16,128]{2,1,0:T(8,128)}) %all-gather.2.cloned.1.call-update) | async-done | bytes 25165840 | tf_op jit(solution)/shard_map/all_gather | solution.py:276
  158.2 1.7 broadcast_in_dim.27.phr_ref
  159.9 1.7 broadcast_in_dim.28.phi_ref
  161.7 0.0 copy-done
  161.7 85.8 %spread.1 = f32[128,32,512]{2,1,0:T(8,128)} custom-call(s32[3072]{0:T(1024)} %get-tuple-element.18.r_ref, s32[3072]{0:T(1024)} %get-tuple-element.17.c_ref, f32[3072,16,128]{2,1,0:T(8,128)} %all-gather.2.cloned.1.call-done.p_ref, f32[128,8,128]{2,1,0:T(8,128)} %broadcast_in_dim.27.phr_ref, f32[128,8,128]{2,1,0:T(8,128)} %broadcast_in_dim.28.phi_ref, ...), custom_call_target="tpu_custom_call" | custom-call | tf_op jit(solution)/shard_map/spread/pallas_call | solution.py:208
  247.4 0.0 copy-start.1
  247.5 10.1 %copy.35 = f32[128,32,512]{0,2,1:T(8,128)} copy(f32[128,32,512]{2,1,0:T(8,128)} %spread.1) | data formatting | bytes 16777216 | tf_op jit(solution)/shard_map/reshape | solution.py:288
  257.5 0.0 copy-done.1
  257.5 7.9 %convolution_bitcast_fusion.1 = f32[128,2,32,256,1]{0,3,1,2,4:T(8,128)} fusion(f32[128,32,2,256,1]{0,3,2,4,1:T(8,128)} %bitcast.36, f32[2,128,2,128,1]{3,1,2,0,4:T(8,128)S(1)} %copy-done.1), kind=kOutput, calls=%fused_computation.1 | convolution fusion | flops 3221225472 | bytes 17039360 | tf_op jit(solution)/shard_map/omcr,ricn->moin/dot_general | solution.py:290
  265.4 10.3 %copy.33 = f32[128,2,32,256,1]{3,2,1,4,0:T(8,128)} copy(f32[128,2,32,256,1]{0,3,1,2,4:T(8,128)} %convolution_bitcast_fusion.1) | data formatting | bytes 16777216 | tf_op jit(solution)/shard_map/omcr,ricn->moin/transpose | solution.py:290
  275.8 8.5 %convolution_bitcast_fusion = f32[2,32,128,256]{3,1,0,2:T(8,128)S(1)} fusion(f32[128,2,32,256,1]{3,2,1,4,0:T(8,128)} %copy.33, f32[128,2,32,2,32]{4,2,3,1,0:T(8,128)} %constant.72.clone), kind=kOutput, calls=%fused_computation | convolution fusion | flops 805306368 | bytes 18874368 | tf_op jit(solution)/shard_map/mpkoi,moin->pkmn/dot_general | solution.py:294
  284.3 8.3 %copy.30 = f32[2,32,128,256]{3,2,1,0:T(8,128)} copy(f32[2,32,128,256]{3,1,0,2:T(8,128)S(1)} %convolution_bitcast_fusion) | data formatting | bytes 16777216 | tf_op jit(solution)/shard_map/mpkoi,moin->pkmn/transpose | solution.py:294
  (10 shorter events, 0.1 us)
Async XLA Ops:
  6.5 151.7 %all-gather.2.cloned.1.call-start = ((), (), s32[]{:S(2)}) async-start(), calls=%async_computation | async-start | bytes 26738688 | tf_op jit(solution)/shard_map/all_gather | solution.py:276
  78.9 82.7 %copy-start = (bf16[256,512]{1,0:T(8,128)(2,1)}, bf16[256,512]{1,0:T(8,128)(2,1)S(1)}, u32[]{:S(2)}) copy-start(bf16[256,512]{1,0:T(8,128)(2,1)S(1)} %broadcast_dynamic-update-slice_fusion.tab_ref) | copy-start | bytes 786436
  247.4 10.1 %copy-start.1 = (f32[2,128,2,128,1]{3,1,2,0,4:T(8,128)S(1)}, f32[2,128,2,128,1]{3,1,2,0,4:T(8,128)}, u32[]{:S(2)}) copy-start(f32[2,128,2,128,1]{3,1,2,0,4:T(8,128)} %constant.79) | copy-start | bytes 786436
Sparse Core Ops, SparseCore 0:
  27.8 130.4 all-gather.1

commit v2 on v1

--- a/solution.py
+++ b/solution.py
@@ -15,6 +15,7 @@
 TILES = GRID // SUB
 F32 = jnp.float32
 BF16 = jnp.bfloat16
+CUTS = (0, 7, 14, 20, 24)
 
 
 def _poly_coefs():
@@ -129,23 +130,45 @@
         grid=(count // block,),
         in_specs=[spec] * 4,
         out_specs=pl.BlockSpec((block, 16, 128), lambda g: (g, 0, 0)),
+        cost_estimate=pl.CostEstimate(
+            flops=count * 64 * 1024 * 64, bytes_accessed=count * 10240, transcendentals=0
+        ),
         name="pixels",
     )(ar, ai, u, v)
 
 
-def spread_kernel(block, nc, r_ref, c_ref, p_ref, phr_ref, phi_ref, tab_ref, x_ref, y_ref):
+def spread_kernel(block, nc, first, last, *refs):
+    refs = list(refs)
+    r_ref, c_ref, p_ref, phr_ref, phi_ref, tab_ref = refs[:6]
+    refs = refs[6:]
+    xin_ref = None if first else refs.pop(0)
+    if last:
+        dft_ref, mix_hbm = refs.pop(0), refs.pop(0)
+    out_hbm, x_ref, y_ref, sem = refs[:4]
+    if last:
+        z_ref, o_ref, mix_ref, mix_sem = refs[4:]
     g = pl.program_id(0)
+    steps = pl.num_programs(0)
     halves = nc // 128
     chunk = 8
     rows = chunk * 16
 
     @pl.when(g == 0)
     def _():
-        def zero(t, carry):
-            x_ref[t] = jnp.zeros(x_ref.shape[1:], F32)
-            return carry
-
-        lax.fori_loop(0, TILES, zero, 0)
+        if last:
+            pltpu.make_async_copy(mix_hbm, mix_ref, mix_sem).start()
+        if first:
+
+            def zero(t, carry):
+                for lt in range(2 * halves):
+                    x_ref[lt, pl.ds(t * 32, 32), :] = jnp.zeros((32, 128), F32)
+                return carry
+
+            lax.fori_loop(0, TILES, zero, 0)
+        else:
+            load = pltpu.make_async_copy(xin_ref, x_ref, sem)
+            load.start()
+            load.wait()
 
     lane = lax.broadcasted_iota(jnp.int32, (rows, 128), 1)
 
@@ -156,12 +179,12 @@
         lof = p - hif
         hir = pltpu.roll(hif, 64, 1)
         lor = pltpu.roll(lof, 64, 1)
-        first = jnp.where(lane < 64, hif, lor).astype(BF16)
-        second = jnp.where(lane < 64, hir, lof).astype(BF16)
+        one = jnp.where(lane < 64, hif, lor).astype(BF16)
+        two = jnp.where(lane < 64, hir, lof).astype(BF16)
         lhs = jnp.concatenate(
             [
-                jnp.concatenate([first, hi], 1),
-                jnp.concatenate([second, hir.astype(BF16)], 1),
+                jnp.concatenate([one, hi], 1),
+                jnp.concatenate([two, hir.astype(BF16)], 1),
             ],
             0,
         )
@@ -177,16 +200,14 @@
             for half in range(2):
                 for sub in range(2):
                     src = half * rows + d * 16 + sub * 8
-                    dst = half * 16 + sub * 8
+                    dst = pl.ds(pl.multiple_of(r * 32 + half * 16 + sub * 8, 8), 8)
                     for n in range(halves):
-                        re = pl.ds(n * 128, 128)
-                        im = pl.ds(nc + n * 128, 128)
-                        yr = y_ref[slot, pl.ds(src, 8), re]
-                        yi = y_ref[slot, pl.ds(src, 8), im]
-                        x_ref[r, pl.ds(dst, 8), re] += yr * pr - yi * pi
-                        x_ref[r, pl.ds(dst, 8), im] += yr * pi + yi * pr
-
-    steps = block // chunk
+                        yr = y_ref[slot, pl.ds(src, 8), pl.ds(n * 128, 128)]
+                        yi = y_ref[slot, pl.ds(src, 8), pl.ds(nc + n * 128, 128)]
+                        x_ref[n, dst, :] += yr * pr - yi * pi
+                        x_ref[halves + n, dst, :] += yr * pi + yi * pr
+
+    trips = block // chunk
     multiply(0, 0)
 
     def body(t, carry):
@@ -196,32 +217,122 @@
         add(2 * t + 1, 1)
         return carry
 
-    lax.fori_loop(0, steps // 2 - 1, body, 0)
-    multiply(steps - 1, 1)
-    add(steps - 2, 0)
-    add(steps - 1, 1)
-
-
-def spread(rows, cols, pix, phr, phi, table, nc, block):
+    lax.fori_loop(0, trips // 2 - 1, body, 0)
+    multiply(trips - 1, 1)
+    add(trips - 2, 0)
+    add(trips - 1, 1)
+
+    @pl.when(g == steps - 1)
+    def _():
+        if not last:
+            store = pltpu.make_async_copy(x_ref, out_hbm, sem)
+            store.start()
+            store.wait()
+            return
+        dot = functools.partial(jnp.dot, preferred_element_type=F32)
+
+        def rows_dft(i, carry):
+            pick = pl.ds(i, TILES, stride=SUB)
+            parts = [
+                jnp.concatenate([x_ref[ri * halves + n, pick, :] for n in range(halves)], 1)
+                for ri in range(2)
+            ]
+            xh, xl = split(jnp.concatenate(parts, 0))
+            wide_dot = dot(dft_ref[...], xh)
+            res = wide_dot[:256] + wide_dot[256:] + dot(dft_ref[:256], xl)
+            for o in range(2):
+                for n in range(halves):
+                    z_ref[o * halves + n, pick, :] = res[
+                        o * 128 : o * 128 + 128, n * 128 : n * 128 + 128
+                    ]
+            return carry
+
+        lax.fori_loop(0, SUB, rows_dft, 0)
+        pltpu.make_async_copy(mix_hbm, mix_ref, mix_sem).wait()
+
+        def mix(m, carry):
+            near = pl.ds(pl.multiple_of(m * SUB, SUB), SUB)
+            far = pl.ds(m, SUB, stride=TILES)
+            zm = jnp.concatenate(
+                [
+                    jnp.concatenate([z_ref[o * halves + n, near, :] for n in range(halves)], 1)
+                    for o in range(2)
+                ],
+                0,
+            )
+            zh, zl = split(zm)
+            res = dot(mix_ref[m], jnp.concatenate([zh, zl, zh], 0))
+            for p in range(2):
+                for n in range(halves):
+                    o_ref[p * halves + n, far, :] = res[
+                        p * 32 : p * 32 + 32, n * 128 : n * 128 + 128
+                    ]
+            return carry
+
+        lax.fori_loop(0, TILES, mix, 0)
+        stores = [
+            pltpu.make_async_copy(
+                o_ref.at[p * halves + n],
+                out_hbm.at[p, :, pl.ds(n * 128, 128)],
+                sem,
+            )
+            for p in range(2)
+            for n in range(halves)
+        ]
+        for store in stores:
+            store.start()
+        for store in stores:
+            store.wait()
+
+
+def spread(rows, cols, pix, phr, phi, table, nc, block, x=None, finish=None):
     count = pix.shape[0]
+    tiles = 2 * nc // 128
     const = lambda shape: pl.BlockSpec(shape, lambda g, r, c: (0,) * len(shape))
+    anywhere = pl.BlockSpec(memory_space=pl.ANY)
+    x_shape = (tiles, GRID, 128)
+    args = [rows, cols, pix, phr, phi, table]
+    specs = [
+        pl.BlockSpec((block, 16, 128), lambda g, r, c: (g, 0, 0)),
+        const((TILES, 8, 128)),
+        const((TILES, 8, 128)),
+        const((256, 2 * nc)),
+    ]
+    scratch = [
+        pltpu.VMEM(x_shape, F32),
+        pltpu.VMEM((2, 256, 2 * nc), F32),
+        pltpu.SemaphoreType.DMA,
+    ]
+    if x is not None:
+        args.append(x)
+        specs.append(anywhere)
+    if finish is None:
+        out = jax.ShapeDtypeStruct(x_shape, F32)
+    else:
+        args.extend(finish)
+        specs.extend([const(finish[0].shape), anywhere])
+        out = jax.ShapeDtypeStruct((2, GRID, nc), F32)
+        scratch += [
+            pltpu.VMEM(x_shape, F32),
+            pltpu.VMEM(x_shape, F32),
+            pltpu.VMEM(finish[1].shape, BF16),
+            pltpu.SemaphoreType.DMA,
+        ]
     return pl.pallas_call(
-        functools.partial(spread_kernel, block, nc),
-        out_shape=jax.ShapeDtypeStruct((TILES, SUB, 2 * nc), F32),
+        functools.partial(spread_kernel, block, nc, x is None, finish is not None),
+        out_shape=out,
         grid_spec=pltpu.PrefetchScalarGridSpec(
             num_scalar_prefetch=2,
             grid=(count // block,),
-            in_specs=[
-                pl.BlockSpec((block, 16, 128), lambda g, r, c: (g, 0, 0)),
-                const((TILES, 8, 128)),
-                const((TILES, 8, 128)),
-                const((256, 2 * nc)),
-            ],
-            out_specs=const((TILES, SUB, 2 * nc)),
-            scratch_shapes=[pltpu.VMEM((2, 256, 2 * nc), F32)],
+            in_specs=specs,
+            out_specs=anywhere,
+            scratch_shapes=scratch,
         ),
-        name="spread",
-    )(rows, cols, pix, phr, phi, table)
+        cost_estimate=pl.CostEstimate(
+            flops=count * 32 * 192 * 4 * nc, bytes_accessed=count * 8192 * 8, transcendentals=0
+        ),
+        name="finish" if finish is not None else "spread",
+    )(*args)
 
 
 def np_split(x):
@@ -264,35 +375,34 @@
     live = jnp.where(
         jnp.arange(VIS)[None, :] < vis_count[:, None], 1.0 / math.sqrt(VIS), 0.0
     )
-    tile = (owner * band + tile_row) * TILES + tile_col
+    subs = visibilities.shape[0]
+    tile = ((owner * band + tile_row) * TILES + tile_col).astype(F32)
+    padded = -(-subs // 1024) * 1024
+    tile = jnp.zeros((padded,), F32).at[:subs].set(tile).reshape(padded // 128, 128)
     tile = lax.all_gather(tile, "wide", tiled=True)
-    pix = pixels(
-        visibilities[:, 0] * live,
-        visibilities[:, 1] * live,
-        offsets[:, 0],
-        offsets[:, 1],
-        64,
-    )
-    pix = lax.all_gather(pix, "wide", tiled=True)
+    tile = tile.reshape(wide, padded)[:, :subs].astype(jnp.int32)
+    real, imag = visibilities[:, 0] * live, visibilities[:, 1] * live
+    off_u, off_v = offsets[:, 0], offsets[:, 1]
+    edges = [subs * k // 24 for k in CUTS]
+    spans = [slice(lo, hi) for lo, hi in zip(edges, edges[1:])]
+    gathered = []
+    for span in spans:
+        pix = pixels(real[span], imag[span], off_u[span], off_v[span], 8)
+        gathered.append(lax.all_gather(pix, "wide", tiled=True))
     spread8 = lambda m: jnp.broadcast_to(jnp.asarray(m, F32)[:, None, :], (TILES, 8, 128))
-    x = spread(
-        tile // TILES,
-        tile % TILES,
-        pix,
-        spread8(w.real),
-        spread8(w.imag),
-        column_table(g, nc),
-        nc,
-        64,
-    )
-    x = x.reshape(TILES, SUB, 2, nc)
-    c4 = jnp.asarray(real_form(w).transpose(0, 2, 1, 3), F32)
-    z = jnp.einsum("omcr,ricn->moin", c4, x, precision=lax.Precision.HIGH)
+    phr, phi = spread8(w.real), spread8(w.imag)
+    table = column_table(g, nc)
+    dh, dl = np_split(real_form(w).transpose(0, 2, 1, 3).reshape(256, 256))
     index = (np.arange(SUB)[:, None] + np.arange(SUB)[None, :]) % SUB
-    m4 = real_form(g[index] / 256.0)
-    m4 = jnp.asarray(m4.transpose(4, 0, 3, 1, 2), F32)
-    out = jnp.einsum("mpkoi,moin->pkmn", m4, z, precision=lax.Precision.HIGH)
-    return out.reshape(2, GRID, nc)
+    m4 = real_form(g[index] / 256.0).transpose(4, 0, 3, 1, 2).reshape(TILES, 64, 64)
+    mh, ml = (jnp.asarray(m) for m in np_split(m4))
+    finish = (jnp.asarray(np.concatenate([dh, dl])), jnp.concatenate([mh, mh, ml], 2))
+    x = None
+    for span, pix in zip(spans, gathered):
+        ids = tile[:, span].reshape(-1)
+        end = finish if span is spans[-1] else None
+        x = spread(ids // TILES, ids % TILES, pix, phr, phi, table, nc, 64, x, end)
+    return x
 
 
 def solution(mesh):

time: 302 us -> 351 us (1.16)
  Pallas kernels: 102 us -> 185 us
  waiting for transfers between devices: 78.6 us -> 116 us
  blocking collectives: 46.7 us -> 16.2 us
  local copies, waits for them, and re-layouts: 38.1 us -> 12.8 us
  matrix products: 16.4 us -> 0 us
    pallas_call x1 -> x4, Pallas kernels: 85.8 us -> 164 us  [spread(): pl.pallas_call(functools.partial(spread_kernel, block, nc, x is None, fin...]
    unnamed x1 -> x0, blocking collectives: 46.7 us -> none
    all_gather x1 -> x4, waiting for transfers between devices: 78.6 us -> 116 us  [per_device(): gathered.append(lax.all_gather(pix, 'wide', tiled=True))]
    transpose x2 -> x0, local copies, waits for them, and re-layouts: 18.6 us -> none  [the longest x1 10.3 us: per_device(): z = jnp.einsum('omcr,ricn->moin', c4, x, precision=lax.Precision.HIGH)]
    dot_general x2 -> x0, matrix products: 16.4 us -> none  [the longest x1 8.49 us: per_device(): out = jnp.einsum('mpkoi,moin->pkmn', m4, z, precision=lax.Precision.HIGH)]
    all_gather x0 -> x1, blocking collectives: none -> 16.2 us  [per_device(): tile = lax.all_gather(tile, 'wide', tiled=True)]
    reshape x1 -> x6, local copies, waits for them, and re-layouts: 10.1 us -> 0.34 us  [the longest x4 0.31 us: per_device(): ids = tile[:, span].reshape(-1)]
    slice x2 -> x12, local copies, waits for them, and re-layouts: 3.06 us -> 9.15 us  [the longest x8 7.71 us: per_device(): pix = pixels(real[span], imag[span], off_u[span], off_v[span], 8)]
  transfers between devices with their start and end apart: 1 -> 4, of which waited for: 1 -> 4; matrix products, arithmetic and copies ran while one was open for 1% -> 4% of each run, Pallas kernels for 0% -> 30%
where the time goes in v2:
time: 351 us; the launch traced here: 348 us
  Pallas kernels  185 us (53%)
  waiting for transfers between devices  116 us (33%)
  blocking collectives  16.2 us (5%)
  between operations  13.3 us (4%)
  local copies, waits for them, and re-layouts  12.8 us (4%)
  other arithmetic  4.02 us (1%)
    pallas_call x4, Pallas kernels, spread(): pl.pallas_call(functools.partial(spread_kernel, block, nc, x is None, fin...  164 us
    all_gather x4, waiting for transfers between devices, per_device(): gathered.append(lax.all_gather(pix, 'wide', tiled=True))  116 us
    pallas_call x4, Pallas kernels, pixels(): pl.pallas_call(functools.partial(pixel_kernel, block), out_shape=jax.Shap...  21.4 us
    all_gather x1, blocking collectives, per_device(): tile = lax.all_gather(tile, 'wide', tiled=True)  16.2 us
    slice x8, local copies, waits for them, and re-layouts, per_device(): pix = pixels(real[span], imag[span], off_u[span], off_v[span], 8)  7.71 us
  transfers between devices with their start and end apart: 4, of which 4 were waited for; matrix products, arithmetic and copies ran while one was open for 4% of the time, Pallas kernels for 30%

profile of v2, /device:TPU:15, one launch (start us, length us, event | category | flops | bytes accessed | tf_op | source)
XLA Modules:
  0.0 347.7 jit_solution(7923739081725686379)
XLA Ops:
  6.5 0.0 copy-start.2
  6.5 0.0 copy-start.1
  6.5 0.0 all-gather.11.cloned.1.call-start
  6.5 1.2 fusion.10
  7.8 1.6 fusion.7
  9.4 0.8 select_multiply_fusion
  10.2 0.7 fusion.11
  10.9 6.1 %pixels.7 = f32[56,16,128]{2,1,0:T(8,128)} custom-call(f32[56,128]{1,0:T(8,128)} %get-tuple-element.52.ar_ref, f32[56,128]{1,0:T(8,128)} %get-tuple-element.27.ai_ref, f32[56,128]{1,0:T(8,128)} %bitcast.37, f32[56,128]{1,0:T(8,128)} %bitcast.36), custom_call_target="tpu_custom_call" | custom-call | flops 234881024 | bytes 573440 | tf_op jit(solution)/shard_map/pixels/pallas_call | solution.py:127
  16.9 0.0 all-gather.11.cloned.1.call-update
  16.9 0.0 all-gather.9.cloned.1.call-start
  17.0 6.0 %pixels.6 = f32[56,16,128]{2,1,0:T(8,128)} custom-call(f32[56,128]{1,0:T(8,128)} %get-tuple-element.51.ar_ref, f32[56,128]{1,0:T(8,128)} %get-tuple-element.28.ai_ref, f32[56,128]{1,0:T(8,128)} %bitcast.35, f32[56,128]{1,0:T(8,128)} %bitcast.34), custom_call_target="tpu_custom_call" | custom-call | flops 234881024 | bytes 573440 | tf_op jit(solution)/shard_map/pixels/pallas_call | solution.py:127
  23.0 0.0 all-gather.9.cloned.1.call-update
  23.0 0.0 all-gather.7.cloned.1.call-start
  23.1 0.6 slice.150.ar_ref
  23.7 0.6 slice.151.ai_ref
  24.3 1.5 fusion.8
  25.8 5.3 %pixels.5 = f32[48,16,128]{2,1,0:T(8,128)} custom-call(f32[48,128]{1,0:T(8,128)} %slice.150.ar_ref, f32[48,128]{1,0:T(8,128)} %slice.151.ai_ref, f32[48,128]{1,0:T(8,128)} %bitcast.39, f32[48,128]{1,0:T(8,128)} %bitcast.38), custom_call_target="tpu_custom_call" | custom-call | flops 201326592 | bytes 491520 | tf_op jit(solution)/shard_map/pixels/pallas_call | solution.py:127
  31.2 0.0 all-gather.7.cloned.1.call-update
  31.2 0.0 all-gather.5.cloned.1.call-start
  31.2 0.6 slice.147.ar_ref
  31.8 0.6 slice.148.ai_ref
  32.4 1.5 fusion.9
  33.9 4.0 %pixels.4 = f32[32,16,128]{2,1,0:T(8,128)} custom-call(f32[32,128]{1,0:T(8,128)} %slice.147.ar_ref, f32[32,128]{1,0:T(8,128)} %slice.148.ai_ref, f32[32,128]{1,0:T(8,128)} %bitcast.41, f32[32,128]{1,0:T(8,128)} %bitcast.40), custom_call_target="tpu_custom_call" | custom-call | flops 134217728 | bytes 327680 | tf_op jit(solution)/shard_map/pixels/pallas_call | solution.py:127
  37.9 0.0 all-gather.5.cloned.1.call-update
  37.9 0.7 add_convert_fusion
  38.6 16.2 %all_gather.15 = f32[128,128]{1,0:T(8,128)S(1)} all-gather(f32[8,128]{1,0:T(8,128)S(1)} %pad_bitcast_fusion), channel_id=1, replica_groups=mesh['group'=2,'wide'=16] {'wide'}, dimensions={0}, use_global_device_ids=true | all-gather | bytes 69632 | tf_op jit(solution)/shard_map/all_gather | solution.py:382
  54.9 0.1 slice.149
  54.9 0.1 slice.146
  55.0 0.1 fusion.13
  55.1 0.1 reshape.56
  55.2 0.1 reshape.55
  55.3 0.1 reshape.54
  55.3 0.1 reshape.53
  55.4 0.8 constant_dynamic-slice_fusion.5
  56.2 0.8 constant_dynamic-slice_fusion.1
  57.1 0.0 copy-start
  57.2 0.6 add_select_fusion.6
  57.8 0.6 add_select_fusion
  58.4 0.6 add_select_fusion.2
  59.0 0.6 add_select_fusion.4
  59.6 26.0 %all-gather.11.cloned.1.call-done.refs_2_ = f32[896,16,128]{2,1,0:T(8,128)} async-done(((f32[56,16,128]{2,1,0:T(8,128)}), f32[896,16,128]{2,1,0:T(8,128)}) %all-gather.11.cloned.1.call-update) | async-done | bytes 7340048 | tf_op jit(solution)/shard_map/all_gather | solution.py:391
  85.7 0.0 copy-done.2
  85.7 0.9 broadcast_in_dim.28.refs_3_
  86.5 0.0 copy-done.1
  86.5 0.8 broadcast_in_dim.29.refs_4_
  87.4 0.0 copy-done
  87.4 29.5 %spread.3.refs_6_ = f32[4,4096,128]{2,1,0:T(8,128)} custom-call(s32[896]{0:T(1024)} %get-tuple-element.42.refs_0_, s32[896]{0:T(1024)} %get-tuple-element.41.refs_1_, f32[896,16,128]{2,1,0:T(8,128)} %all-gather.11.cloned.1.call-done.refs_2_, f32[128,8,128]{2,1,0:T(8,128)} %broadcast_in_dim.28.refs_3_, f32[128,8,128]{2,1,0:T(8,128)} %broadcast_in_dim.29.refs_4_, ...), custom_call_target="tpu_custom_call" | custom-call | flops 5637144576 | bytes 58720256 | tf_op jit(solution)/shard_map/spread/pallas_call | solution.py:321
  116.9 37.4 %all-gather.9.cloned.1.call-done.refs_2_ = f32[896,16,128]{2,1,0:T(8,128)} async-done(((f32[56,16,128]{2,1,0:T(8,128)}), f32[896,16,128]{2,1,0:T(8,128)}) %all-gather.9.cloned.1.call-update) | async-done | bytes 7340048 | tf_op jit(solution)/shard_map/all_gather | solution.py:391
  154.3 32.3 %spread.4.refs_6_ = f32[4,4096,128]{2,1,0:T(8,128)} custom-call(s32[896]{0:T(1024)} %get-tuple-element.44.refs_0_, s32[896]{0:T(1024)} %get-tuple-element.43.refs_1_, f32[896,16,128]{2,1,0:T(8,128)} %all-gather.9.cloned.1.call-done.refs_2_, f32[128,8,128]{2,1,0:T(8,128)} %broadcast_in_dim.28.refs_3_, f32[128,8,128]{2,1,0:T(8,128)} %broadcast_in_dim.29.refs_4_, ...), custom_call_target="tpu_custom_call" | custom-call | flops 5637144576 | bytes 58720256 | tf_op jit(solution)/shard_map/spread/pallas_call | solution.py:321
  186.7 30.3 %all-gather.7.cloned.1.call-done.refs_2_ = f32[768,16,128]{2,1,0:T(8,128)} async-done(((f32[48,16,128]{2,1,0:T(8,128)}), f32[768,16,128]{2,1,0:T(8,128)}) %all-gather.7.cloned.1.call-update) | async-done | bytes 6291472 | tf_op jit(solution)/shard_map/all_gather | solution.py:391
  216.9 28.8 %spread.5.refs_6_ = f32[4,4096,128]{2,1,0:T(8,128)} custom-call(s32[768]{0:T(1024)} %get-tuple-element.46.refs_0_, s32[768]{0:T(1024)} %get-tuple-element.45.refs_1_, f32[768,16,128]{2,1,0:T(8,128)} %all-gather.7.cloned.1.call-done.refs_2_, f32[128,8,128]{2,1,0:T(8,128)} %broadcast_in_dim.28.refs_3_, f32[128,8,128]{2,1,0:T(8,128)} %broadcast_in_dim.29.refs_4_, ...), custom_call_target="tpu_custom_call" | custom-call | flops 4831838208 | bytes 50331648 | tf_op jit(solution)/shard_map/spread/pallas_call | solution.py:321
  245.7 22.4 %all-gather.5.cloned.1.call-done.refs_2_ = f32[512,16,128]{2,1,0:T(8,128)} async-done(((f32[32,16,128]{2,1,0:T(8,128)}), f32[512,16,128]{2,1,0:T(8,128)}) %all-gather.5.cloned.1.call-update) | async-done | bytes 4194320 | tf_op jit(solution)/shard_map/all_gather | solution.py:391
  268.1 73.0 %finish.1 = f32[2,4096,256]{2,1,0:T(8,128)} custom-call(s32[512]{0:T(512)} %get-tuple-element.48.refs_0_, s32[512]{0:T(512)} %get-tuple-element.47.refs_1_, f32[512,16,128]{2,1,0:T(8,128)} %all-gather.5.cloned.1.call-done.refs_2_, f32[128,8,128]{2,1,0:T(8,128)} %broadcast_in_dim.28.refs_3_, f32[128,8,128]{2,1,0:T(8,128)} %broadcast_in_dim.29.refs_4_, ...), custom_call_target="tpu_custom_call" | custom-call | flops 3221225472 | bytes 33554432 | tf_op jit(solution)/shard_map/finish/pallas_call | solution.py:321
  (12 shorter events, 0.1 us)
Async XLA Ops:
  6.5 79.1 %copy-start.2 = (f32[128,128]{1,0:T(8,128)S(1)}, f32[128,128]{1,0:T(8,128)}, u32[]{:S(2)}) copy-start(f32[128,128]{1,0:T(8,128)} %constant.137.clone) | copy-start | bytes 196612
  6.5 80.0 %copy-start.1 = (f32[128,128]{1,0:T(8,128)S(1)}, f32[128,128]{1,0:T(8,128)}, u32[]{:S(2)}) copy-start(f32[128,128]{1,0:T(8,128)} %constant.138.clone) | copy-start | bytes 196612
  6.5 79.1 %all-gather.11.cloned.1.call-start = ((), (), s32[]{:S(2)}) async-start(), calls=%async_computation.3 | async-start | bytes 7798784 | tf_op jit(solution)/shard_map/all_gather | solution.py:391
  16.9 137.4 %all-gather.9.cloned.1.call-start = ((), (), s32[]{:S(2)}) async-start(), calls=%async_computation.2 | async-start | bytes 7798784 | tf_op jit(solution)/shard_map/all_gather | solution.py:391
  23.0 193.9 %all-gather.7.cloned.1.call-start = ((), (), s32[]{:S(2)}) async-start(), calls=%async_computation.1 | async-start | bytes 6684672 | tf_op jit(solution)/shard_map/all_gather | solution.py:391
  31.2 236.9 %all-gather.5.cloned.1.call-start = ((), (), s32[]{:S(2)}) async-start(), calls=%async_computation | async-start | bytes 4456448 | tf_op jit(solution)/shard_map/all_gather | solution.py:391
  57.1 30.2 %copy-start = (bf16[256,512]{1,0:T(8,128)(2,1)}, bf16[256,512]{1,0:T(8,128)(2,1)S(1)}, u32[]{:S(2)}) copy-start(bf16[256,512]{1,0:T(8,128)(2,1)S(1)} %broadcast_dynamic-update-slice_fusion.refs_5_) | copy-start | bytes 786436
Sparse Core Ops, SparseCore 0:
  17.1 68.5 all-gather.10
  88.0 66.3 all-gather.8
  156.6 60.2 all-gather.6
  218.9 49.1 all-gather.4

commit v3 on v2

--- a/solution.py
+++ b/solution.py
@@ -15,7 +15,6 @@
 TILES = GRID // SUB
 F32 = jnp.float32
 BF16 = jnp.bfloat16
-CUTS = (0, 7, 14, 20, 24)
 
 
 def _poly_coefs():
@@ -121,20 +120,23 @@
     lax.fori_loop(0, block // 4, body, 0)
 
 
-def pixels(ar, ai, u, v, block):
-    count = ar.shape[0]
-    spec = pl.BlockSpec((block, VIS), lambda g: (g, 0))
+def pixels(raw, block, count):
+    devices = raw.shape[0]
+    turns = count // block
+    spec = lambda q: pl.BlockSpec((None, block, VIS), lambda d, t: (d, q * turns + t, 0))
     return pl.pallas_call(
         functools.partial(pixel_kernel, block),
-        out_shape=jax.ShapeDtypeStruct((count, 16, 128), F32),
-        grid=(count // block,),
-        in_specs=[spec] * 4,
-        out_specs=pl.BlockSpec((block, 16, 128), lambda g: (g, 0, 0)),
+        out_shape=jax.ShapeDtypeStruct((devices * count, 16, 128), F32),
+        grid=(devices, turns),
+        in_specs=[spec(q) for q in range(4)],
+        out_specs=pl.BlockSpec((block, 16, 128), lambda d, t: (d * turns + t, 0, 0)),
         cost_estimate=pl.CostEstimate(
-            flops=count * 64 * 1024 * 64, bytes_accessed=count * 10240, transcendentals=0
+            flops=devices * count * 64 * 1024 * 64,
+            bytes_accessed=devices * count * 10240,
+            transcendentals=0,
         ),
         name="pixels",
-    )(ar, ai, u, v)
+    )(raw, raw, raw, raw)
 
 
 def spread_kernel(block, nc, first, last, *refs):
@@ -197,15 +199,18 @@
             c = c_ref[s]
             pr = phr_ref[c]
             pi = phi_ref[c]
-            for half in range(2):
-                for sub in range(2):
-                    src = half * rows + d * 16 + sub * 8
-                    dst = pl.ds(pl.multiple_of(r * 32 + half * 16 + sub * 8, 8), 8)
-                    for n in range(halves):
-                        yr = y_ref[slot, pl.ds(src, 8), pl.ds(n * 128, 128)]
-                        yi = y_ref[slot, pl.ds(src, 8), pl.ds(nc + n * 128, 128)]
-                        x_ref[n, dst, :] += yr * pr - yi * pi
-                        x_ref[halves + n, dst, :] += yr * pi + yi * pr
+            dst = pl.ds(pl.multiple_of(r * 32, 32), 32)
+            old = x_ref[:, dst, :]
+            tops = y_ref[slot, pl.ds(d * 16, 16), :]
+            bots = y_ref[slot, pl.ds(rows + d * 16, 16), :]
+            y = jnp.concatenate([tops, bots], 0)
+            real, imag = [], []
+            for n in range(halves):
+                yr = y[:, n * 128 : n * 128 + 128].reshape(4, 8, 128)
+                yi = y[:, nc + n * 128 : nc + n * 128 + 128].reshape(4, 8, 128)
+                real.append((yr * pr - yi * pi).reshape(1, 32, 128))
+                imag.append((yr * pi + yi * pr).reshape(1, 32, 128))
+            x_ref[:, dst, :] = old + jnp.concatenate(real + imag, 0)
 
     trips = block // chunk
     multiply(0, 0)
@@ -247,7 +252,7 @@
                     ]
             return carry
 
-        lax.fori_loop(0, SUB, rows_dft, 0)
+        lax.fori_loop(0, SUB, rows_dft, 0, unroll=2)
         pltpu.make_async_copy(mix_hbm, mix_ref, mix_sem).wait()
 
         def mix(m, carry):
@@ -269,7 +274,7 @@
                     ]
             return carry
 
-        lax.fori_loop(0, TILES, mix, 0)
+        lax.fori_loop(0, TILES, mix, 0, unroll=8)
         stores = [
             pltpu.make_async_copy(
                 o_ref.at[p * halves + n],
@@ -376,19 +381,23 @@
         jnp.arange(VIS)[None, :] < vis_count[:, None], 1.0 / math.sqrt(VIS), 0.0
     )
     subs = visibilities.shape[0]
+    cut = subs // 4
     tile = ((owner * band + tile_row) * TILES + tile_col).astype(F32)
     padded = -(-subs // 1024) * 1024
     tile = jnp.zeros((padded,), F32).at[:subs].set(tile).reshape(padded // 128, 128)
-    tile = lax.all_gather(tile, "wide", tiled=True)
-    tile = tile.reshape(wide, padded)[:, :subs].astype(jnp.int32)
-    real, imag = visibilities[:, 0] * live, visibilities[:, 1] * live
-    off_u, off_v = offsets[:, 0], offsets[:, 1]
-    edges = [subs * k // 24 for k in CUTS]
-    spans = [slice(lo, hi) for lo, hi in zip(edges, edges[1:])]
-    gathered = []
-    for span in spans:
-        pix = pixels(real[span], imag[span], off_u[span], off_v[span], 8)
-        gathered.append(lax.all_gather(pix, "wide", tiled=True))
+    parts = [
+        visibilities[:, 0] * live,
+        visibilities[:, 1] * live,
+        offsets[:, 0],
+        offsets[:, 1],
+    ]
+    raw = jnp.concatenate([p[:cut] for p in parts] + [tile], 0)
+    raw = lax.all_gather(raw[None], "wide", tiled=True)
+    own = jnp.concatenate([p[cut:] for p in parts], 0)[None]
+    pix = lax.all_gather(pixels(own, cut, subs - cut), "wide", tiled=True)
+    tile = raw[:, 4 * cut :].reshape(wide, padded)[:, :subs].astype(jnp.int32)
+    gathered = [pixels(raw, cut, cut), pix]
+    spans = [slice(0, cut), slice(cut, subs)]
     spread8 = lambda m: jnp.broadcast_to(jnp.asarray(m, F32)[:, None, :], (TILES, 8, 128))
     phr, phi = spread8(w.real), spread8(w.imag)
     table = column_table(g, nc)

time: 351 us -> 254 us (0.72)
  waiting for transfers between devices: 116 us -> 32.5 us
  blocking collectives: 16.2 us -> 0 us
  Pallas kernels: 185 us -> 194 us
  local copies, waits for them, and re-layouts: 12.8 us -> 8.3 us
    all_gather x4 -> x2, waiting for transfers between devices: 116 us -> 32.5 us  [the longest x1 23.3 us: per_device(): raw = lax.all_gather(raw[None], 'wide', tiled=True)]
    pallas_call x4 -> x2, Pallas kernels: 21.4 us -> 74.6 us  [pixels(): pl.pallas_call(functools.partial(pixel_kernel, block), out_shape=jax.Shap...]
    pallas_call x4 -> x2, Pallas kernels: 164 us -> 119 us  [spread(): pl.pallas_call(functools.partial(spread_kernel, block, nc, x is None, fin...]
    all_gather x1 -> x0, blocking collectives: 16.2 us -> none  [per_device(): tile = lax.all_gather(tile, 'wide', tiled=True)]
    slice x9 -> x6, local copies, waits for them, and re-layouts: 8.94 us -> 4.09 us  [the longest x1 1.19 us: per_device(): visibilities[:, 1] * live]
  transfers between devices with their start and end apart: 4 -> 2, of which waited for: 4 -> 2; matrix products, arithmetic and copies ran while one was open for 4% -> 3% of each run, Pallas kernels for 30% -> 40%
where the time goes in v3:
time: 254 us; the launch traced here: 252 us
  Pallas kernels  194 us (76%)
  waiting for transfers between devices  32.5 us (13%)
  between operations  13.6 us (5%)
  local copies, waits for them, and re-layouts  8.3 us (3%)
  other arithmetic  3.51 us (1%)
    pallas_call x2, Pallas kernels, spread(): pl.pallas_call(functools.partial(spread_kernel, block, nc, x is None, fin...  119 us
    pallas_call x2, Pallas kernels, pixels(): pl.pallas_call(functools.partial(pixel_kernel, block), out_shape=jax.Shap...  74.6 us
    all_gather x1, waiting for transfers between devices, per_device(): raw = lax.all_gather(raw[None], 'wide', tiled=True)  23.3 us
    all_gather x1, waiting for transfers between devices, per_device(): pix = lax.all_gather(pixels(own, cut, subs - cut), 'wide', tiled=True)  9.16 us
  transfers between devices with their start and end apart: 2, of which 2 were waited for; matrix products, arithmetic and copies ran while one was open for 3% of the time, Pallas kernels for 40%

profile of v3, /device:TPU:15, one launch (start us, length us, event | category | flops | bytes accessed | tf_op | source)
XLA Modules:
  0.0 252.0 jit_solution(730882327259687810)
XLA Ops:
  6.5 0.0 all-gather.6.cloned.1.call-start
  6.5 0.9 fusion.5
  7.5 1.2 fusion.6
  8.7 0.8 select_multiply_fusion
  9.5 0.7 add_convert_fusion
  10.2 0.0 copy-start
  10.2 0.6 copy-done
  10.8 0.0 all-gather.6.cloned.1.call-update
  10.9 0.0 all-gather.4.cloned.1.call-start
  11.0 1.1 fusion.4
  12.1 0.7 maximum_bitcast_fusion.ar_ref.ai_ref.u_ref.v_ref
  12.8 12.8 %pixels.2 = f32[144,16,128]{2,1,0:T(8,128)} custom-call(f32[1,576,128]{2,1,0:T(8,128)} %maximum_bitcast_fusion.ar_ref.ai_ref.u_ref.v_ref, f32[1,576,128]{2,1,0:T(8,128)} %maximum_bitcast_fusion.ar_ref.ai_ref.u_ref.v_ref, f32[1,576,128]{2,1,0:T(8,128)} %maximum_bitcast_fusion.ar_ref.ai_ref.u_ref.v_ref, ...), custom_call_target="tpu_custom_call" | custom-call | flops 603979776 | bytes 1474560 | tf_op jit(solution)/shard_map/pixels/pallas_call | solution.py:127
  25.6 0.0 all-gather.4.cloned.1.call-update
  25.7 0.8 constant_dynamic-slice_fusion.5
  26.5 0.8 constant_dynamic-slice_fusion.1
  27.4 0.0 copy-start.3
  27.4 23.3 %all-gather.6.cloned.1.call-done = f32[3200,128]{1,0:T(8,128)} async-done(((f32[200,128]{1,0:T(8,128)}), f32[3200,128]{1,0:T(8,128)}) %all-gather.6.cloned.1.call-update) | async-done | bytes 1638416 | tf_op jit(solution)/shard_map/all_gather | solution.py:395
  50.8 0.8 slice.91
  51.7 0.1 slice.93
  51.7 0.1 reshape.44
  51.8 0.1 reshape.43
  51.9 0.6 add_select_fusion.2
  52.5 0.6 add_select_fusion
  53.1 0.0 copy-start.2
  53.1 0.0 copy-start.1
  53.1 61.7 %pixels.3.refs_2_ = f32[768,16,128]{2,1,0:T(8,128)} custom-call(f32[16,200,128]{2,1,0:T(8,128)} %bitcast.28, f32[16,200,128]{2,1,0:T(8,128)} %bitcast.29, f32[16,200,128]{2,1,0:T(8,128)} %bitcast.30, f32[16,200,128]{2,1,0:T(8,128)} %bitcast.31), custom_call_target="tpu_custom_call" | custom-call | flops 3221225472 | bytes 7864320 | tf_op jit(solution)/shard_map/pixels/pallas_call | solution.py:127
  114.8 0.0 copy-done.3
  114.8 0.0 copy-done.2
  114.8 0.8 broadcast_in_dim.36.refs_3_
  115.7 0.0 copy-done.1
  115.7 0.8 broadcast_in_dim.37.refs_4_
  116.5 26.0 %spread.1.refs_6_ = f32[4,4096,128]{2,1,0:T(8,128)} custom-call(s32[768]{0:T(1024)} %get-tuple-element.34.refs_0_, s32[768]{0:T(1024)} %get-tuple-element.33.refs_1_, f32[768,16,128]{2,1,0:T(8,128)} %pixels.3.refs_2_, f32[128,8,128]{2,1,0:T(8,128)} %broadcast_in_dim.36.refs_3_, f32[128,8,128]{2,1,0:T(8,128)} %broadcast_in_dim.37.refs_4_, ...), custom_call_target="tpu_custom_call" | custom-call | flops 4831838208 | bytes 50331648 | tf_op jit(solution)/shard_map/spread/pallas_call | solution.py:326
  142.5 9.2 %all-gather.4.cloned.1.call-done.refs_2_ = f32[2304,16,128]{2,1,0:T(8,128)} async-done(((f32[144,16,128]{2,1,0:T(8,128)}), f32[2304,16,128]{2,1,0:T(8,128)}) %all-gather.4.cloned.1.call-update) | async-done | bytes 18874384 | tf_op jit(solution)/shard_map/all_gather | solution.py:397
  151.7 93.5 %finish.1 = f32[2,4096,256]{2,1,0:T(8,128)} custom-call(s32[2304]{0:T(1024)} %get-tuple-element.32.refs_0_, s32[2304]{0:T(1024)} %get-tuple-element.31.refs_1_, f32[2304,16,128]{2,1,0:T(8,128)} %all-gather.4.cloned.1.call-done.refs_2_, f32[128,8,128]{2,1,0:T(8,128)} %broadcast_in_dim.36.refs_3_, f32[128,8,128]{2,1,0:T(8,128)} %broadcast_in_dim.37.refs_4_, ...), custom_call_target="tpu_custom_call" | custom-call | flops 14495514624 | bytes 150994944 | tf_op jit(solution)/shard_map/finish/pallas_call | solution.py:326
  (19 shorter events, 0.1 us)
Async XLA Ops:
  6.5 44.2 %all-gather.6.cloned.1.call-start = ((), (), s32[]{:S(2)}) async-start(), calls=%async_computation.1 | async-start | bytes 1740800 | tf_op jit(solution)/shard_map/all_gather | solution.py:395
  10.2 0.6 copy-start
  10.9 140.8 %all-gather.4.cloned.1.call-start = ((), (), s32[]{:S(2)}) async-start(), calls=%async_computation | async-start | bytes 20054016 | tf_op jit(solution)/shard_map/all_gather | solution.py:397
  27.4 87.4 %copy-start.3 = (bf16[256,512]{1,0:T(8,128)(2,1)}, bf16[256,512]{1,0:T(8,128)(2,1)S(1)}, u32[]{:S(2)}) copy-start(bf16[256,512]{1,0:T(8,128)(2,1)S(1)} %broadcast_dynamic-update-slice_fusion.refs_5_) | copy-start | bytes 786436
  53.1 61.7 %copy-start.2 = (f32[128,128]{1,0:T(8,128)S(1)}, f32[128,128]{1,0:T(8,128)}, u32[]{:S(2)}) copy-start(f32[128,128]{1,0:T(8,128)} %constant.108.clone) | copy-start | bytes 196612
  53.1 62.6 %copy-start.1 = (f32[128,128]{1,0:T(8,128)S(1)}, f32[128,128]{1,0:T(8,128)}, u32[]{:S(2)}) copy-start(f32[128,128]{1,0:T(8,128)} %constant.109.clone) | copy-start | bytes 196612
Sparse Core Ops, SparseCore 0:
  11.0 39.7 all-gather.5
  52.4 99.2 all-gather.3
